TPU v7x, 256 devices: a whole 4x4x8 slice. The times are simulated.
256 devices in a mesh: frame: 16 (over z_hi, y), space: 16 (over z_lo, x, core).
Axes of the slice: x: 4, y: 4, z: 8 (z_hi: 4, z_lo: 2; z = z_hi * 2 + z_lo), core: 2. Of those that a mesh axis runs over, the one named last changes fastest.
Arguments:
- hidden_in: bfloat16 [2, 16, 32, 64, 1152], P(None, 'frame', 'space'), may hold values from -6 to 6
- attn_cotangent: bfloat16 [2, 16, 32, 64, 1152], P(None, 'frame', 'space'), may hold values from -6 to 6
- w_qkv: bfloat16 [1152, 3456], P('space'), may hold values from -0.1875 to 0.1875
- modulation_table: bfloat16 [1000, 2, 1152], replicated, may hold values from -3 to 3
- snr_table: float32 [1000], replicated, may hold values from 0.1 to 1
- timestep: int32 [2], replicated, may hold values from 0 to 999
- weight_index: int32 [2], replicated, may hold values from 0 to 999
Outputs:
- grad_input: bfloat16 [2, 16, 32, 64, 1152], P(None, 'frame', 'space')
- grad_w_qkv: float32 [1152, 3456], P('space')
- grad_modulation: float32 [2, 2, 1152], replicated
All inputs are finite; a program needn't handle non-finite values.
Results may differ from a plain program's by a relative error of at most 0.029.
Values may be sent and summed in bfloat16 or wider, within the bound.
A program may use at most 128 MiB of HBM per device.

v0:
```python
import jax
import jax.numpy as jnp
from jax import lax
from jax.sharding import PartitionSpec as P

HEADS = 16
HEAD_DIM = 72


def attend_back(queries, keys, values, upstream):
    factor = queries.shape[-1] ** (-0.5)
    queries = queries.astype(jnp.float32)
    keys = keys.astype(jnp.float32)
    values = values.astype(jnp.float32)
    upstream = upstream.astype(jnp.float32)
    highest = lax.Precision.HIGHEST
    scores = jnp.einsum("bfxhe,bgxhe->bxhfg", queries, keys, precision=highest) * factor
    expd = jnp.exp(scores)
    probs = expd / jnp.sum(expd, axis=-1, keepdims=True)
    grad_probs = jnp.einsum("bfxhe,bgxhe->bxhfg", upstream, values, precision=highest)
    grad_values = jnp.einsum("bxhfg,bfxhe->bgxhe", probs, upstream, precision=highest)
    grad_scores = probs * (grad_probs - jnp.sum(probs * grad_probs, axis=-1, keepdims=True))
    grad_queries = jnp.einsum("bxhfg,bgxhe->bfxhe", grad_scores, keys, precision=highest) * factor
    grad_keys = jnp.einsum("bxhfg,bfxhe->bgxhe", grad_scores, queries, precision=highest) * factor
    return (
        grad_queries.astype(jnp.bfloat16),
        grad_keys.astype(jnp.bfloat16),
        grad_values.astype(jnp.bfloat16),
    )


def per_device(
    hidden_in, attn_cotangent, w_qkv, modulation_table, snr_table, timestep, weight_index
):
    clip_count, frame_dev, row_dev, col_count, model_width = hidden_in.shape
    positions = row_dev * col_count
    values_in = hidden_in.astype(jnp.float32)
    average = jnp.mean(values_in, axis=-1, keepdims=True)
    centered = values_in - average
    variance = jnp.mean(centered * centered, axis=-1, keepdims=True)
    inverse_std = lax.rsqrt(variance + 1e-06)
    normed = centered * inverse_std
    modulation = modulation_table[timestep].astype(jnp.float32)
    shift = modulation[:, 0][:, None, None, None, :]
    scale = modulation[:, 1][:, None, None, None, :]
    modulated = (normed * (1.0 + scale) + shift).astype(jnp.bfloat16)
    mod_rows = modulated.reshape(-1, model_width)
    w_full = lax.all_gather(w_qkv, "space", axis=0, tiled=True)
    projected = jnp.dot(mod_rows, w_full, preferred_element_type=jnp.float32).astype(jnp.bfloat16)
    projected = projected.reshape(clip_count, frame_dev, positions, 3, model_width)
    loss_weight = snr_table[weight_index]
    upstream = (loss_weight[:, None, None, None, None] * attn_cotangent.astype(jnp.float32)).astype(
        jnp.bfloat16
    )
    upstream = upstream.reshape(clip_count, frame_dev, positions, 1, model_width)
    packed = jnp.concatenate([projected, upstream], axis=3)
    received = lax.all_to_all(packed, "frame", split_axis=2, concat_axis=1, tiled=True)
    item_count = received.shape[0]
    frames = received.shape[1]
    across = received.shape[2]
    pieces = received.reshape(item_count, frames, across, 4, HEADS, HEAD_DIM)
    head_grads = attend_back(
        pieces[:, :, :, 0], pieces[:, :, :, 1], pieces[:, :, :, 2], pieces[:, :, :, 3]
    )
    stacked = jnp.stack(head_grads, axis=3).reshape(item_count, frames, across, 3, model_width)
    grad_projected = lax.all_to_all(stacked, "frame", split_axis=1, concat_axis=2, tiled=True)
    grad_rows = grad_projected.reshape(-1, 3 * model_width)
    device_count = lax.axis_size("frame") * lax.axis_size("space")
    grad_scale_factor = float(mod_rows.shape[0] * device_count) ** (-0.5)
    row_share = lax.psum_scatter(
        lax.dot_general(
            mod_rows, grad_rows, (((0,), (0,)), ((), ())), preferred_element_type=jnp.float32
        ).astype(jnp.bfloat16),
        "space",
        scatter_dimension=0,
        tiled=True,
    )
    grad_weight = lax.psum(row_share, "frame").astype(jnp.float32) * grad_scale_factor
    grad_hidden = lax.dot_general(
        grad_rows, w_full, (((1,), (1,)), ((), ())), preferred_element_type=jnp.float32
    )
    grad_hidden = grad_hidden.reshape(values_in.shape)
    local_sums = jnp.stack(
        [jnp.sum(grad_hidden, axis=(1, 2, 3)), jnp.sum(grad_hidden * normed, axis=(1, 2, 3))],
        axis=1,
    )
    grad_modulation = lax.psum(local_sums, ("frame", "space")) * grad_scale_factor
    grad_normed = grad_hidden * (1.0 + scale)
    grad_input = (
        grad_normed
        - jnp.mean(grad_normed, axis=-1, keepdims=True)
        - normed * jnp.mean(grad_normed * normed, axis=-1, keepdims=True)
    ) * inverse_std
    return (grad_input.astype(jnp.bfloat16), grad_weight, grad_modulation)


def solution(mesh):
    in_specs = (
        P(None, "frame", "space", None, None),
        P(None, "frame", "space", None, None),
        P("space", None),
        P(),
        P(),
        P(),
        P(),
    )
    out_specs = (P(None, "frame", "space", None, None), P("space", None), P())
    return jax.shard_map(
        per_device, mesh=mesh, in_specs=in_specs, out_specs=out_specs, check_vma=False
    )
```

profile of v0, /device:TPU:2, one launch (start us, length us, event | category | flops | bytes accessed | tf_op | source)
XLA Modules:
  0.0 491.3 jit_solution(7075564899825200032)
XLA Ops:
  8.6 2.9 gather_fusion
  15.6 49.8 %all-gather.2.cloned.1.call-done = bf16[1152,3456]{1,0:T(8,128)(2,1)} async-done(((bf16[72,3456]{1,0:T(8,128)(2,1)}), bf16[1152,3456]{1,0:T(8,128)(2,1)}) %all-gather.2.cloned.1.call-update) | async-done | bytes 7962640 | tf_op jit(solution)/shard_map/all_gather | solution.py:48
  65.5 7.1 %convolution_convert_fusion.1 = bf16[256,3456]{1,0:T(8,128)(2,1)} fusion(bf16[256,1152]{1,0:T(8,128)(2,1)S(1)} %bitcast.76, bf16[1152,3456]{1,0:T(8,128)(2,1)} %all-gather.2.cloned.1.call-done), kind=kOutput, calls=%fused_computation.3 | convolution fusion | flops 2039316480 | bytes 10321920 | tf_op jit(solution)/shard_map/dot_general | solution.py:49
  72.6 2.6 copy.63
  75.2 2.0 reshape.124
  77.2 4.6 pad_maximum_fusion
  81.8 4.9 copy.66
  86.7 67.7 %all_to_all.8 = bf16[2,1,128,4,1152]{4,3,1,0,2:T(4,128)(2,1)S(1)} all-to-all(bf16[2,1,128,4,1152]{4,3,1,0,2:T(4,128)(2,1)} %copy.66), channel_id=1, replica_groups=mesh['frame'=16,'space'=16] {'frame'}, dimensions={2} | all-to-all | bytes 4718592 | tf_op jit(solution)/shard_map/all_to_all | solution.py:57
  154.4 8.8 %reshape.148 = bf16[2,16,8,4,16,72]{5,4,3,0,2,1:T(8,128)(2,1)} reshape(bf16[2,1,128,4,1152]{4,3,1,0,2:T(4,128)(2,1)S(1)} %all_to_all.8) | data formatting | bytes 4718592 | tf_op jit(solution)/shard_map/reshape | solution.py:61
  163.2 3.6 fusion.25
  166.8 1.7 fusion.1
  168.5 1.8 multiply_reduce_fusion
  170.2 2.4 fusion.9
  172.7 2.2 fusion.10
  174.9 3.0 fusion.8
  178.2 1.5 stack.21
  181.4 1.5 copy.75
  184.6 40.6 %all_to_all.9 = bf16[2,16,8,3,1152]{4,2,0,3,1:T(8,128)(2,1)S(1)} all-to-all(bf16[2,16,8,3,1152]{4,2,0,3,1:T(8,128)(2,1)S(1)} %copy.76), channel_id=1, replica_groups=mesh['frame'=16,'space'=16] {'frame'}, dimensions={1} | all-to-all | bytes 3538944 | tf_op jit(solution)/shard_map/all_to_all | solution.py:66
  227.2 5.5 %convolution_convert_fusion = bf16[1152,3456]{1,0:T(8,128)(2,1)} fusion(bf16[256,1152]{1,0:T(8,128)(2,1)S(1)} %bitcast.77, bf16[256,3456]{1,0:T(8,128)(2,1)S(1)} %bitcast.73), kind=kOutput, calls=%fused_computation.2 | convolution fusion | flops 2042413056 | bytes 10321920 | tf_op jit(solution)/shard_map/dot_general | solution.py:71
  232.8 6.5 %fusion.19 = (f32[256]{0:T(256)}, f32[256,1152]{1,0:T(8,128)S(1)}) fusion(f32[2,1152]{1,0:T(2,128)S(1)} %bitcast.80, bf16[256,3456]{1,0:T(8,128)(2,1)S(1)} %bitcast.74, bf16[1152,3456]{1,0:T(8,128)(2,1)} %all-gather.2.cloned.1.call-done), kind=kOutput, calls=%fused_computation.34 | convolution fusion | flops 2039021312 | bytes 10921984 | tf_op jit(solution)/shard_map/dot_general | solution.py:79
  240.6 77.9 %psum.15 = f32[2,2,1152]{2,0,1:T(2,128)S(1)} all-reduce(f32[2,2,1152]{2,0,1:T(2,128)S(1)} %pad_maximum_fusion.2), channel_id=1, replica_groups=mesh['frame'=16,'space'=16] {'frame','space'}, use_global_device_ids=true, to_apply=%region_10.0 | all-reduce | flops 4608 | bytes 36864 | tf_op jit(solution)/shard_map/psum | solution.py:87
  319.3 1.9 fusion.16
  321.2 161.5 %all-reduce.3.cloned.1.call-done = bf16[72,3456]{1,0:T(8,128)(2,1)} async-done(((bf16[72,3456]{1,0:T(8,128)(2,1)}), bf16[72,3456]{1,0:T(8,128)(2,1)}) %all-reduce.3.cloned.1.call-update) | async-done | bytes 497680 | tf_op jit(solution)/shard_map/psum | solution.py:78
  482.7 2.0 convert_multiply_fusion
  (58 shorter events, 13.1 us)
Async XLA Ops:
  7.2 5.1 %copy-start = (f32[1000]{0:T(1024)S(1)}, f32[1000]{0:T(1024)}, u32[]{:S(2)}) copy-start(f32[1000]{0:T(1024)} %param.11) | copy-start | bytes 12004
  7.2 7.6 %copy-start.2 = (bf16[2,1,2,64,1152]{4,3,2,1,0:T(8,128)(2,1)S(1)}, bf16[2,1,2,64,1152]{4,3,2,1,0:T(8,128)(2,1)}, u32[]{:S(2)}) copy-start(bf16[2,1,2,64,1152]{4,3,2,1,0:T(8,128)(2,1)} %param.7) | copy-start | bytes 1769476
  7.2 58.3 %all-gather.2.cloned.1.call-start = ((), (), s32[]{:S(2)}) async-start(), calls=%async_computation.3 | async-start | bytes 8460288 | tf_op jit(solution)/shard_map/all_gather | solution.py:48
  7.9 311.4 %reduce-scatter.5.cloned.1.call-start = ((), (), s32[]{:S(2)}) async-start(), calls=%async_computation.5 | async-start | bytes 8460288
  15.0 224.4 %copy-start.5 = (f32[2,2,64]{2,1,0:T(2,128)}, f32[2,2,64]{2,1,0:T(2,128)S(1)}, u32[]{:S(2)}) copy-start(f32[2,2,64]{2,1,0:T(2,128)S(1)} %broadcast_multiply_fusion.2) | copy-start | bytes 3076
  15.3 50.2 %copy-start.6 = (f32[2,2,64]{2,1,0:T(2,128)}, f32[2,2,64]{2,1,0:T(2,128)S(1)}, u32[]{:S(2)}) copy-start(f32[2,2,64]{2,1,0:T(2,128)S(1)} %add_rsqrt_fusion) | copy-start | bytes 3076
  15.6 49.8 %copy-start.3 = (bf16[2,1,2,64,1152]{4,3,2,1,0:T(8,128)(2,1)}, bf16[2,1,2,64,1152]{4,3,2,1,0:T(8,128)(2,1)S(1)}, u32[]{:S(2)}) copy-start(bf16[2,1,2,64,1152]{4,3,2,1,0:T(8,128)(2,1)S(1)} %fusion.12) | copy-start | bytes 1769476
  226.1 1.1 copy-start.4
  232.7 250.0 %all-reduce.3.cloned.1.call-start = ((), (), s32[]{:S(2)}) async-start(), calls=%async_computation.4 | async-start | bytes 995328 | tf_op jit(solution)/shard_map/psum | solution.py:78
  239.3 79.9 %copy-start.8 = (f32[256]{0:T(256)S(1)}, f32[256]{0:T(256)}, u32[]{:S(2)}) copy-start(f32[256]{0:T(256)} %get-tuple-element.25) | copy-start | bytes 3076
  239.4 79.9 %copy-start.7 = (f32[2,2,64]{2,1,0:T(2,128)S(1)}, f32[2,2,64]{2,1,0:T(2,128)}, u32[]{:S(2)}) copy-start(f32[2,2,64]{2,1,0:T(2,128)} %copy-done.6) | copy-start | bytes 3076
  319.3 165.5 %copy-start.1 = (f32[1000]{0:T(1024)S(1)}, f32[1000]{0:T(1024)}, u32[]{:S(2)}) copy-start(f32[1000]{0:T(1024)} %param.11) | copy-start | bytes 12004
Sparse Core Ops, SparseCore 0:
  9.9 55.5 all-gather.1
  232.9 74.6 reduce-scatter.4
  319.4 163.2 all-reduce.2
where the time goes:
time: 492 us; the launch traced here: 491 us
  waiting for transfers between devices  212 us (43%)
  blocking collectives  186 us (38%)
  local copies, waits for them, and re-layouts  35.1 us (7%)
  matrix products  30.3 us (6%)
  between operations  14 us (3%)
  other arithmetic  13.4 us (3%)
    psum x1, waiting for transfers between devices, per_device(): lax.psum(row_share, 'frame').astype(jnp.float32) * grad_scale_factor  162 us
    psum x1, blocking collectives, per_device(): lax.psum(local_sums, ('frame', 'space')) * grad_scale_factor  77.9 us
    all_to_all x1, blocking collectives, per_device(): lax.all_to_all(packed, 'frame', split_axis=2, concat_axis=1, tiled=True)  67.7 us
    all_gather x1, waiting for transfers between devices, per_device(): w_full = lax.all_gather(w_qkv, 'space', axis=0, tiled=True)  49.8 us
    all_to_all x1, blocking collectives, per_device(): lax.all_to_all(stacked, 'frame', split_axis=1, concat_axis=2, tiled=True)  40.6 us
  transfers between devices with their start and end apart: 3, of which 2 were waited for; matrix products, arithmetic and copies ran while one was open for 4% of the time, Pallas kernels for 0%

commit v1 on v0

--- a/solution.py
+++ b/solution.py
@@ -84,7 +84,9 @@
         [jnp.sum(grad_hidden, axis=(1, 2, 3)), jnp.sum(grad_hidden * normed, axis=(1, 2, 3))],
         axis=1,
     )
-    grad_modulation = lax.psum(local_sums, ("frame", "space")) * grad_scale_factor
+    grad_modulation = (
+        jnp.sum(lax.all_gather(local_sums, ("frame", "space")), axis=0) * grad_scale_factor
+    )
     grad_normed = grad_hidden * (1.0 + scale)
     grad_input = (
         grad_normed

time: 492 us -> 903 us (1.84)
  waiting for transfers between devices: 212 us -> 698 us
  blocking collectives: 186 us -> 108 us
    all_gather x0 -> x1, waiting for transfers between devices: none -> 419 us  [per_device(): lax.all_gather(local_sums, ('frame', 'space'))]
    psum x1 -> x0, blocking collectives: 77.9 us -> none  [per_device(): lax.psum(local_sums, ('frame', 'space')) * grad_scale_factor]
    unnamed x4 -> x5, waiting for transfers between devices: 0.72 us -> 67.3 us
  transfers between devices with their start and end apart: 3 -> 4, of which waited for: 2 -> 4; matrix products, arithmetic and copies ran while one was open for 4% -> 2% of each run, Pallas kernels for 0% -> 0%
where the time goes in v1:
time: 903 us
  waiting for transfers between devices  698 us (77%)
  blocking collectives  108 us (12%)
  local copies, waits for them, and re-layouts  34.5 us (4%)
  matrix products  30.3 us (3%)
  other arithmetic  17 us (2%)
  between operations  14 us (2%)
    all_gather x1, waiting for transfers between devices, per_device(): lax.all_gather(local_sums, ('frame', 'space'))  419 us
    psum x1, waiting for transfers between devices, per_device(): lax.psum(row_share, 'frame').astype(jnp.float32) * grad_scale_factor  162 us
    all_to_all x1, blocking collectives, per_device(): lax.all_to_all(packed, 'frame', split_axis=2, concat_axis=1, tiled=True)  67.7 us
    unnamed x5, waiting for transfers between devices  67.3 us
    all_gather x1, waiting for transfers between devices, per_device(): w_full = lax.all_gather(w_qkv, 'space', axis=0, tiled=True)  49.8 us
    all_to_all x1, blocking collectives, per_device(): lax.all_to_all(stacked, 'frame', split_axis=1, concat_axis=2, tiled=True)  40.6 us
  transfers between devices with their start and end apart: 4, of which 4 were waited for; matrix products, arithmetic and copies ran while one was open for 2% of the time, Pallas kernels for 0%

profile of v1, /device:TPU:2, one launch (start us, length us, event | category | flops | bytes accessed | tf_op | source)
XLA Modules:
  0.0 902.6 jit_solution(12030092307996121918)
XLA Ops:
  8.6 2.9 gather_fusion
  15.6 49.8 %all-gather.4.cloned.1.call-done = bf16[1152,3456]{1,0:T(8,128)(2,1)} async-done(((bf16[72,3456]{1,0:T(8,128)(2,1)}), bf16[1152,3456]{1,0:T(8,128)(2,1)}) %all-gather.4.cloned.1.call-update) | async-done | bytes 7962640 | tf_op jit(solution)/shard_map/all_gather | solution.py:48
  65.5 7.1 convolution_convert_fusion.1
  72.6 2.6 copy.60
  75.2 2.0 reshape.124
  77.2 4.6 pad_maximum_fusion
  81.8 4.9 copy.63
  86.7 67.7 %all_to_all.8 = bf16[2,1,128,4,1152]{4,3,1,0,2:T(4,128)(2,1)S(1)} all-to-all(bf16[2,1,128,4,1152]{4,3,1,0,2:T(4,128)(2,1)} %copy.63), channel_id=1, replica_groups=mesh['frame'=16,'space'=16] {'frame'}, dimensions={2} | all-to-all | bytes 4718592 | tf_op jit(solution)/shard_map/all_to_all | solution.py:57
  154.4 8.8 reshape.149
  163.2 3.6 fusion.25
  166.8 1.7 fusion.1
  168.5 1.8 multiply_reduce_fusion
  170.2 2.4 fusion.9
  172.7 2.2 fusion.10
  174.9 3.0 fusion.8
  178.2 1.5 stack.21
  184.6 40.6 %all_to_all.9 = bf16[2,16,8,3,1152]{4,2,0,3,1:T(8,128)(2,1)S(1)} all-to-all(bf16[2,16,8,3,1152]{4,2,0,3,1:T(8,128)(2,1)S(1)} %copy.73), channel_id=1, replica_groups=mesh['frame'=16,'space'=16] {'frame'}, dimensions={1} | all-to-all | bytes 3538944 | tf_op jit(solution)/shard_map/all_to_all | solution.py:66
  227.2 5.5 convolution_convert_fusion
  232.8 6.5 fusion.19
  240.7 66.6 %reduce-scatter.5.cloned.1.call-done = bf16[72,3456]{1,0:T(8,128)(2,1)} async-done(((bf16[1152,3456]{1,0:T(8,128)(2,1)}), bf16[72,3456]{1,0:T(8,128)(2,1)}) %reduce-scatter.5.cloned.1.call-update) | async-done | bytes 497680
  308.6 419.0 %all-gather.6.cloned.1.call-done = f32[512,2,1152]{2,1,0:T(2,128)} async-done(((f32[2,2,1152]{2,1,0:T(2,128)}), f32[512,2,1152]{2,1,0:T(2,128)}) %all-gather.6.cloned.1.call-update) | async-done | bytes 4718608 | tf_op jit(solution)/shard_map/all_gather | solution.py:88
  727.6 3.7 reduce_sum.89
  731.9 162.2 %all-reduce.3.cloned.1.call-done = bf16[72,3456]{1,0:T(8,128)(2,1)} async-done(((bf16[72,3456]{1,0:T(8,128)(2,1)}), bf16[72,3456]{1,0:T(8,128)(2,1)}) %all-reduce.3.cloned.1.call-update) | async-done | bytes 497680 | tf_op jit(solution)/shard_map/psum | solution.py:78
  894.0 2.0 convert_multiply_fusion
  (62 shorter events, 15.8 us)
Async XLA Ops:
  7.2 5.1 copy-start
  7.2 7.6 copy-start.2
  7.2 58.3 %all-gather.4.cloned.1.call-start = ((), (), s32[]{:S(2)}) async-start(), calls=%async_computation.3 | async-start | bytes 8460288 | tf_op jit(solution)/shard_map/all_gather | solution.py:48
  7.9 299.3 %reduce-scatter.5.cloned.1.call-start = ((), (), s32[]{:S(2)}) async-start(), calls=%async_computation.6 | async-start | bytes 8460288
  15.3 50.2 %copy-start.5 = (f32[2,2,64]{2,1,0:T(2,128)}, f32[2,2,64]{2,1,0:T(2,128)S(1)}, u32[]{:S(2)}) copy-start(f32[2,2,64]{2,1,0:T(2,128)S(1)} %add_rsqrt_fusion) | copy-start | bytes 3076
  15.6 49.8 %copy-start.3 = (bf16[2,1,2,64,1152]{4,3,2,1,0:T(8,128)(2,1)}, bf16[2,1,2,64,1152]{4,3,2,1,0:T(8,128)(2,1)S(1)}, u32[]{:S(2)}) copy-start(bf16[2,1,2,64,1152]{4,3,2,1,0:T(8,128)(2,1)S(1)} %fusion.12) | copy-start | bytes 1769476
  226.1 1.1 copy-start.4
  232.7 494.8 %all-gather.6.cloned.1.call-start = ((), (), s32[]{:S(2)}) async-start(), calls=%async_computation.5 | async-start | bytes 4737024 | tf_op jit(solution)/shard_map/all_gather | solution.py:88
  232.8 6.5 copy-start.6
  239.3 1.3 copy-start.8
  239.3 68.0 %copy-start.7 = (f32[2,2,64]{2,1,0:T(2,128)S(1)}, f32[2,2,64]{2,1,0:T(2,128)}, u32[]{:S(2)}) copy-start(f32[2,2,64]{2,1,0:T(2,128)} %copy-done.5) | copy-start | bytes 3076
  240.5 653.5 %all-reduce.3.cloned.1.call-start = ((), (), s32[]{:S(2)}) async-start(), calls=%async_computation.4 | async-start | bytes 995328 | tf_op jit(solution)/shard_map/psum | solution.py:78
  727.6 168.5 %copy-start.1 = (f32[1000]{0:T(1024)S(1)}, f32[1000]{0:T(1024)}, u32[]{:S(2)}) copy-start(f32[1000]{0:T(1024)} %param.11) | copy-start | bytes 12004
Sparse Core Ops, SparseCore 0:
  9.9 55.5 all-gather.3
  232.9 74.3 reduce-scatter.4
  309.7 417.7 all-gather.5
  730.1 163.9 all-reduce.2
